TPU v7x, 32 devices: a whole 2x2x4 slice. The times are simulated.
32 devices in a mesh: row: 8 (over y, x, core), col: 4 (over z).
Axes of the slice: x: 2, y: 2, z: 4, core: 2. Of those that a mesh axis runs over, the one named last changes fastest.
Arguments:
- panel: bfloat16 [24576, 256], P('row', 'col'), as said below
- trailing: bfloat16 [24576, 16384], P('row', 'col'), may hold values from -6 to 6
- tile_list: int32 [176], P('row'), may hold values from 0 to 23, as said below
Outputs:
- triangle: float32 [256, 256], replicated
- top_rows: float32 [16384, 256], P('col')
- updated: bfloat16 [22528, 16384], P('row', 'col')
Inputs may be any that keep to these rules, and one draw needn't show every extreme that they name: `tile_list`: each aligned block of 22 entries (the entries of one index of row) lists distinct tile numbers of that group's 24 tiles in increasing order and always includes tile 24 - 1. `panel`: the active rows of every row group, and all active rows together, have full column rank with a condition number under 100.
All inputs are finite; a program needn't handle non-finite values.
Results may differ from a plain program's by a relative error of at most 0.0065.
Values may be sent and summed in bfloat16 or wider, within the bound.
No kernel may reach another device: no remote copies, remote signals or barrier semaphores. Data moves between devices by JAX's collectives and lax.ppermute only.
A program may use at most 128 MiB of HBM per device.

v0:
```python
import jax
import jax.numpy as jnp
from jax import lax
from jax.sharding import PartitionSpec as P

TILE = 128


def pick_tiles(whole, tile_list):
    tiled = whole.reshape(-1, TILE, whole.shape[1])
    return jnp.take(tiled, tile_list, axis=0).reshape(-1, whole.shape[1])


def local(panel, trailing, tile_list):
    panel_full = lax.all_gather(panel, "col", axis=1, tiled=True)
    act_panel = pick_tiles(panel_full, tile_list)
    act_trail = pick_tiles(trailing, tile_list)
    local_gram = lax.dot_general(
        act_panel, act_panel, (((0,), (0,)), ((), ())), preferred_element_type=jnp.float32
    )
    gram_matrix = lax.psum(local_gram.astype(jnp.bfloat16), "row").astype(jnp.float32)
    lower_factor = jnp.linalg.cholesky(gram_matrix)
    triangle = lower_factor.T
    local_cross = lax.dot_general(
        act_trail, act_panel, (((0,), (0,)), ((), ())), preferred_element_type=jnp.float32
    )
    cross_sum = lax.psum(local_cross, "row")
    top_rows = jax.scipy.linalg.solve_triangular(lower_factor, cross_sum.T, lower=True).T
    coeff = jax.scipy.linalg.solve_triangular(
        lower_factor, top_rows.T, lower=True, trans=1
    ).T.astype(jnp.bfloat16)
    product = lax.dot_general(
        act_panel, coeff, (((1,), (1,)), ((), ())), preferred_element_type=jnp.float32
    )
    updated = (act_trail.astype(jnp.float32) - product).astype(jnp.bfloat16)
    return (triangle, top_rows, updated)


def solution(mesh):
    return jax.shard_map(
        local,
        mesh=mesh,
        in_specs=(P("row", "col"), P("row", "col"), P("row")),
        out_specs=(P(), P("col", None), P("row", "col")),
        check_vma=False,
    )
```

profile of v0, /device:TPU:0, one launch (start us, length us, event | category | flops | bytes accessed | tf_op | source)
XLA Modules:
  0.0 239.5 jit_solution(15465657170109536758)
XLA Ops:
  7.2 0.0 all-gather.2.cloned.1.call-start
  7.2 0.7 all-gather.2.cloned.1.call-update
  7.9 0.0 all-reduce.4.cloned.1.call-start
  7.9 0.7 compare_and_fusion
  8.6 0.7 compare_select_fusion
  9.3 0.1 broadcast_bitcast_fusion
  9.4 17.7 %gather_fusion.1 = bf16[22,128,4096]{2,1,0:T(8,128)(2,1)} fusion(bf16[24,128,4096]{2,1,0:T(8,128)(2,1)} %bitcast.57, s32[1024]{0:T(1024)S(1)} %pad_clamp_fusion), kind=kCustom, calls=%fused_computation.1 | custom fusion | bytes 46137432 | tf_op jit(solution)/shard_map/jit(_take)/gather | solution.py:11
  27.1 20.6 %bitcast_select_fusion = bf16[2816,4096]{1,0:T(8,128)(2,1)} fusion(bf16[22,128,4096]{2,1,0:T(8,128)(2,1)} %gather_fusion.1, pred[2816]{0:T(1024)(128)(4,1)S(1)} %broadcast_bitcast_fusion), kind=kLoop, calls=%fused_computation.5 | loop fusion | flops 11534336 | bytes 46140160 | tf_op jit(solution)/shard_map/jit(_take)/select_n | solution.py:11
  47.7 1.6 all-gather.2.cloned.1.call-done
  49.3 1.7 copy.11
  51.0 0.6 gather_fusion
  51.7 1.5 fusion.12
  53.1 0.0 all-reduce.4.cloned.1.call-update
  53.2 0.0 all-reduce.6.cloned.1.call-start
  53.2 12.2 %fusion.4 = f32[256,4096]{1,0:T(8,128)} fusion(bf16[22,128,4096]{2,1,0:T(8,128)(2,1)} %gather_fusion.1, pred[22]{0:T(512)(128)(4,1)S(1)} %compare_and_fusion, bf16[22,128,256]{2,1,0:T(8,128)(2,1)S(1)} %gather_fusion), kind=kOutput, calls=%fused_computation.10 | convolution fusion | flops 5917835264 | bytes 28704790 | tf_op jit(solution)/shard_map/dot_general | solution.py:24
  65.4 0.0 all-reduce.6.cloned.1.call-update
  65.4 1.7 bitcast_select_fusion.1
  67.1 40.8 %all-reduce.4.cloned.1.call-done = bf16[256,256]{0,1:T(8,128)(2,1)} async-done(((bf16[256,256]{0,1:T(8,128)(2,1)}), bf16[256,256]{0,1:T(8,128)(2,1)}) %all-reduce.4.cloned.1.call-update) | async-done | bytes 131088 | tf_op jit(solution)/shard_map/psum | solution.py:21
  107.9 1.0 copy.14
  108.9 0.9 fusion.13
  109.9 11.7 %cholesky.50 = f32[128,128]{1,0:T(8,128)S(1)} custom-call(f32[128,128]{1,0:T(8,128)S(1)} %cholesky.118), custom_call_target="Cholesky" | custom-call | tf_op jit(solution)/shard_map/jit(cholesky)/cholesky | solution.py:22
  121.6 9.8 %custom-call.18 = f32[1,128,128]{1,2,0:T(8,128)S(1)} custom-call(f32[1,128,128]{2,1,0:T(8,128)S(1)} %get-tuple-element.32), custom_call_target="InvertDiagBlocksLowerTriangular" | custom-call | tf_op jit(solution)/shard_map/jit(cholesky)/cholesky | solution.py:22
  131.5 0.2 constant_dynamic-update-slice_fusion.1
  131.7 0.3 convolution_subtract_fusion.2
  131.9 11.7 %cholesky.105 = f32[128,128]{1,0:T(8,128)S(1)} custom-call(f32[128,128]{1,0:T(8,128)S(1)} %convolution_subtract_fusion.2), custom_call_target="Cholesky" | custom-call | tf_op jit(solution)/shard_map/jit(cholesky)/cholesky | solution.py:22
  143.7 0.6 compare_reduce_fusion
  145.7 0.8 copy.16
  146.5 0.1 triangular_solve.53
  146.6 4.0 %while.1 = (s32[]{:T(128)}, f32[256,256]{1,0:T(8,128)S(1)}, s32[2,2]{1,0:T(2,128)S(1)}, f32[2,128,128]{2,1,0:T(8,128)S(1)}, s32[]{:T(128)}) while((s32[]{:T(128)}, f32[256,256]{1,0:T(8,128)S(1)}, s32[2,2]{1,0:T(2,128)S(1)}, f32[2,128,128]{2,1,0:T(8,128)S(1)}, s32[]{:T(128)}) %tuple.31), condition=%wide.while_cond, body=%wide.while_body.sunk | while | flops 2 | bytes 131189 | solution.py:28
  146.6 0.6 fusion.37
  147.2 1.4 bitcast_dynamic-update-slice_fusion.2
  148.6 0.6 fusion.37
  149.2 1.4 bitcast_dynamic-update-slice_fusion.2
  150.6 19.9 %custom-call.19 = f32[2,128,128]{1,2,0:T(8,128)S(1)} custom-call(f32[2,128,128]{2,1,0:T(8,128)S(1)} %get-tuple-element.10), custom_call_target="InvertDiagBlocksLowerTriangular" | custom-call | tf_op jit(solution)/shard_map/jit(_solve_triangular)/triangular_solve | solution.py:28
  170.5 0.0 copy-start.1
  170.5 21.7 %all-reduce.6.cloned.1.call-done = f32[256,4096]{1,0:T(8,128)} async-done(((f32[256,4096]{1,0:T(8,128)}), f32[256,4096]{1,0:T(8,128)}) %all-reduce.6.cloned.1.call-update) | async-done | bytes 4194320 | tf_op jit(solution)/shard_map/psum | solution.py:27
  192.2 0.0 copy-start
  192.2 3.6 %fusion.7 = f32[128,4096]{1,0:T(8,128)S(1)} fusion(f32[256,4096]{1,0:T(8,128)} %all-reduce.6.cloned.1.call-done, f32[2,128,128]{1,2,0:T(8,128)S(1)} %custom-call.19), kind=kOutput, calls=%fused_computation.15 | convolution fusion | flops 805306368 | bytes 4259840 | tf_op jit(solution)/shard_map/jit(_solve_triangular)/triangular_solve | solution.py:28
  195.9 0.0 copy-done
  195.9 1.9 convolution_subtract_fusion.1
  197.8 1.9 fusion.20
  199.8 0.0 copy-done.1
  199.8 1.9 fusion.27
  201.7 2.5 %maximum_bitcast_fusion = f32[4096,256]{0,1:T(8,128)} fusion(f32[128,4096]{1,0:T(8,128)S(1)} %fusion.20, f32[128,4096]{1,0:T(8,128)S(1)} %fusion.7), kind=kLoop, calls=%fused_computation.14 | loop fusion | flops 1048576 | bytes 8388608 | tf_op jit(solution)/shard_map/transpose | solution.py:28
  204.2 0.0 copy-start.2
  204.2 2.0 convolution_subtract_fusion
  206.1 0.0 copy-done.2
  206.2 1.9 convolution_convert_fusion
  208.1 5.9 %copy.17 = f32[4096,256]{1,0:T(8,128)} copy(f32[4096,256]{0,1:T(8,128)} %maximum_bitcast_fusion) | data formatting | bytes 8388608
  213.9 19.1 %subtract_convert_fusion = bf16[2816,4096]{1,0:T(8,128)(2,1)} fusion(bf16[2816,4096]{1,0:T(8,128)(2,1)} %bitcast_select_fusion, bf16[2816,256]{1,0:T(8,128)(2,1)S(1)} %bitcast_select_fusion.1, bf16[128,4096]{1,0:T(8,128)(2,1)S(1)} %get-tuple-element.35, bf16[128,4096]{1,0:T(8,128)(2,1)S(1)} %convolution_convert_fusion), kind=kOutput, calls=%fused_computation.4 | convolution fusion | flops 5944377344 | bytes 49676288 | tf_op jit(solution)/shard_map/dot_general | solution.py:32
  (10 shorter events, 0.2 us)
Async XLA Ops:
  7.2 42.2 %all-gather.2.cloned.1.call-start = ((), (), s32[]{:S(2)}) async-start(), calls=%async_computation | async-start | bytes 1966080 | tf_op jit(solution)/shard_map/all_gather | solution.py:15
  7.9 100.0 %all-reduce.4.cloned.1.call-start = ((), (), s32[]{:S(2)}) async-start(), calls=%async_computation.1 | async-start | bytes 262144 | tf_op jit(solution)/shard_map/psum | solution.py:21
  53.2 139.0 %all-reduce.6.cloned.1.call-start = ((), (), s32[]{:S(2)}) async-start(), calls=%async_computation.2 | async-start | bytes 8388608 | tf_op jit(solution)/shard_map/psum | solution.py:27
  170.5 29.2 %copy-start.1 = (f32[2,128,128]{1,2,0:T(8,128)}, f32[2,128,128]{1,2,0:T(8,128)S(1)}, u32[]{:S(2)}) copy-start(f32[2,128,128]{1,2,0:T(8,128)S(1)} %custom-call.19) | copy-start | bytes 393220
  192.2 3.7 %copy-start = (f32[256,4096]{1,0:T(8,128)S(1)}, f32[256,4096]{1,0:T(8,128)}, u32[]{:S(2)}) copy-start(f32[256,4096]{1,0:T(8,128)} %all-reduce.6.cloned.1.call-done) | copy-start | bytes 12582916
  204.2 2.0 copy-start.2
Sparse Core Ops, SparseCore 0:
  9.5 39.7 all-gather.1
  53.3 54.5 all-reduce.3
  111.7 80.4 all-reduce.5
where the time goes:
time: 240 us
  other arithmetic  80.9 us (34%)
  waiting for transfers between devices  64.8 us (27%)
  matrix products  46.5 us (19%)
  local copies, waits for them, and re-layouts  31.9 us (13%)
  between operations  15.2 us (6%)
    psum x1, waiting for transfers between devices, local(): lax.psum(local_gram.astype(jnp.bfloat16), 'row').astype(jnp.float32)  40.8 us
    another operation x6, other arithmetic, local(): lower_factor = jnp.linalg.cholesky(gram_matrix)  34 us
    select_n x3, other arithmetic, pick_tiles(): return jnp.take(tiled, tile_list, axis=0).reshape(-1, whole.shape[1])  22.9 us
    psum x1, waiting for transfers between devices, local(): cross_sum = lax.psum(local_cross, 'row')  21.7 us
    another operation x3, other arithmetic, local(): jax.scipy.linalg.solve_triangular(lower_factor, cross_sum.T, lower=True)  19.9 us
    dot_general x1, matrix products, local(): lax.dot_general(act_panel, coeff, (((1,), (1,)), ((), ())), preferred_ele...  19.1 us
    gather x2, local copies, waits for them, and re-layouts, pick_tiles(): return jnp.take(tiled, tile_list, axis=0).reshape(-1, whole.shape[1])  18.4 us
    dot_general x1, matrix products, local(): lax.dot_general(act_trail, act_panel, (((0,), (0,)), ((), ())), preferred...  12.2 us
  transfers between devices with their start and end apart: 3, of which 3 were waited for; matrix products, arithmetic and copies ran while one was open for 48% of the time, Pallas kernels for 0%

commit v1 on v0

--- a/solution.py
+++ b/solution.py
@@ -1,9 +1,28 @@
+import functools
 import jax
 import jax.numpy as jnp
 from jax import lax
 from jax.sharding import PartitionSpec as P
+from jax.lax import axis_size, ppermute
 
 TILE = 128
+
+
+def work_trails(patch, axis_id):
+    extent = axis_size(axis_id)
+
+    def handle_rings(item_now, parts_out):
+        if parts_out >= extent:
+            return item_now
+        copies = []
+        for b in range(extent):
+            copies.append((b, b ^ parts_out))
+        return handle_rings(item_now + ppermute(item_now, axis_id, copies), 2 * parts_out)
+
+    return handle_rings(patch, 1)
+
+
+obtain_thing = functools.partial(work_trails, axis_id="row")
 
 
 def pick_tiles(whole, tile_list):
@@ -24,7 +43,7 @@
     local_cross = lax.dot_general(
         act_trail, act_panel, (((0,), (0,)), ((), ())), preferred_element_type=jnp.float32
     )
-    cross_sum = lax.psum(local_cross, "row")
+    cross_sum = obtain_thing(local_cross)
     top_rows = jax.scipy.linalg.solve_triangular(lower_factor, cross_sum.T, lower=True).T
     coeff = jax.scipy.linalg.solve_triangular(
         lower_factor, top_rows.T, lower=True, trans=1

time: 240 us -> 363 us (1.51); the launches traced: 240 us -> 356 us
  waiting for transfers between devices: 64.8 us -> 172 us
  other arithmetic: 80.9 us -> 87.4 us
    ppermute x0 -> x3, waiting for transfers between devices: none -> 98.2 us  [handle_rings(): ppermute(item_now, axis_id, copies)]
    psum x1 -> x0, waiting for transfers between devices: 21.7 us -> none  [local(): cross_sum = lax.psum(local_cross, 'row')]
    all_gather x1, waiting for transfers between devices: 1.63 us -> 23 us  [local(): panel_full = lax.all_gather(panel, 'col', axis=1, tiled=True)]
    psum x1, waiting for transfers between devices: 40.8 us -> 49.8 us  [local(): lax.psum(local_gram.astype(jnp.bfloat16), 'row').astype(jnp.float32)]
    transpose x0 -> x1, other arithmetic: none -> 4.04 us  [local(): top_rows = jax.scipy.linalg.solve_triangular(lower_factor, cross_sum.T, l...]
  transfers between devices with their start and end apart: 3 -> 5, of which waited for: 3 -> 4; matrix products, arithmetic and copies ran while one was open for 48% -> 29% of each run, Pallas kernels for 0% -> 0%
where the time goes in v1:
time: 363 us; the launch traced here: 356 us
  waiting for transfers between devices  172 us (47%)
  other arithmetic  87.4 us (24%)
  matrix products  46.4 us (13%)
  local copies, waits for them, and re-layouts  31.5 us (9%)
  between operations  15.8 us (4%)
    ppermute x3, waiting for transfers between devices, handle_rings(): ppermute(item_now, axis_id, copies)  98.2 us
    psum x1, waiting for transfers between devices, local(): lax.psum(local_gram.astype(jnp.bfloat16), 'row').astype(jnp.float32)  49.8 us
    another operation x6, other arithmetic, local(): lower_factor = jnp.linalg.cholesky(gram_matrix)  34 us
    select_n x3, other arithmetic, pick_tiles(): return jnp.take(tiled, tile_list, axis=0).reshape(-1, whole.shape[1])  23.2 us
    all_gather x1, waiting for transfers between devices, local(): panel_full = lax.all_gather(panel, 'col', axis=1, tiled=True)  23 us
    another operation x3, other arithmetic, local(): jax.scipy.linalg.solve_triangular(lower_factor, cross_sum.T, lower=True)  19.9 us
    dot_general x1, matrix products, local(): lax.dot_general(act_panel, coeff, (((1,), (1,)), ((), ())), preferred_ele...  19.1 us
    gather x2, local copies, waits for them, and re-layouts, pick_tiles(): return jnp.take(tiled, tile_list, axis=0).reshape(-1, whole.shape[1])  18.4 us
  transfers between devices with their start and end apart: 5, of which 4 were waited for; matrix products, arithmetic and copies ran while one was open for 29% of the time, Pallas kernels for 0%

profile of v1, /device:TPU:0, one launch (start us, length us, event | category | flops | bytes accessed | tf_op | source)
XLA Modules:
  0.0 355.9 jit_solution(15178598162428567197)
XLA Ops:
  7.2 0.0 all-gather.2.cloned.1.call-start
  7.2 0.7 all-gather.2.cloned.1.call-update
  7.9 0.0 all-reduce.3.cloned.1.call-start
  7.9 0.7 compare_select_fusion
  8.6 0.0 copy-start.2
  8.6 17.7 %gather_fusion.1 = bf16[22,128,4096]{2,1,0:T(8,128)(2,1)} fusion(bf16[24,128,4096]{2,1,0:T(8,128)(2,1)} %bitcast.58, s32[1024]{0:T(1024)S(1)} %pad_clamp_fusion), kind=kCustom, calls=%fused_computation.1 | custom fusion | bytes 46137432 | tf_op jit(solution)/shard_map/jit(_take)/gather | solution.py:30
  26.4 0.0 copy-done.2
  26.4 23.0 %all-gather.2.cloned.1.call-done = bf16[3072,256]{0,1:T(8,128)(2,1)} async-done(((bf16[3072,64]{0,1:T(8,128)(2,1)}), bf16[3072,256]{0,1:T(8,128)(2,1)}) %all-gather.2.cloned.1.call-update) | async-done | bytes 1572880 | tf_op jit(solution)/shard_map/all_gather | solution.py:34
  49.3 1.7 copy.12
  51.0 0.6 gather_fusion
  51.7 11.9 %fusion.4 = f32[4096,256]{1,0:T(8,128)S(1)} fusion(bf16[22,128,4096]{2,1,0:T(8,128)(2,1)} %gather_fusion.1, pred[22]{0:T(512)(128)(4,1)S(1)} %compare_and_fusion, bf16[22,128,256]{2,1,0:T(8,128)(2,1)S(1)} %gather_fusion), kind=kOutput, calls=%fused_computation.10 | convolution fusion | flops 5917835264 | bytes 28704790 | tf_op jit(solution)/shard_map/dot_general | solution.py:43
  63.5 0.1 collective-permute-start
  63.6 7.1 %collective-permute-done = f32[4096,256]{1,0:T(8,128)S(1)} collective-permute-done((f32[4096,256]{1,0:T(8,128)S(1)}, f32[4096,256]{1,0:T(8,128)S(1)}, u32[]{:S(2)}, u32[]{:S(2)}) %collective-permute-start) | collective-permute-done | bytes 4194336 | tf_op jit(solution)/shard_map/ppermute | solution.py:20
  70.8 0.5 add.45
  71.3 1.5 collective-permute-start.1
  72.9 0.1 broadcast_bitcast_fusion
  72.9 91.1 %collective-permute-done.1 = f32[4096,256]{1,0:T(8,128)S(1)} collective-permute-done((f32[4096,256]{1,0:T(8,128)S(1)}, f32[4096,256]{1,0:T(8,128)S(1)}, u32[]{:S(2)}, u32[]{:S(2)}) %collective-permute-start.1) | collective-permute-done | bytes 4194336 | tf_op jit(solution)/shard_map/ppermute | solution.py:20
  164.0 2.6 add.46
  166.5 1.5 collective-permute-start.2
  168.0 20.6 %bitcast_select_fusion = bf16[2816,4096]{1,0:T(8,128)(2,1)} fusion(bf16[22,128,4096]{2,1,0:T(8,128)(2,1)} %gather_fusion.1, pred[2816]{0:T(1024)(128)(4,1)S(1)} %broadcast_bitcast_fusion), kind=kLoop, calls=%fused_computation.5 | loop fusion | flops 11534336 | bytes 46140160 | tf_op jit(solution)/shard_map/jit(_take)/select_n | solution.py:30
  188.6 1.5 fusion.13
  190.1 0.0 all-reduce.3.cloned.1.call-update
  190.1 1.9 bitcast_select_fusion.1
  192.0 49.8 %all-reduce.3.cloned.1.call-done = bf16[256,256]{0,1:T(8,128)(2,1)} async-done(((bf16[256,256]{0,1:T(8,128)(2,1)}), bf16[256,256]{0,1:T(8,128)(2,1)}) %all-reduce.3.cloned.1.call-update) | async-done | bytes 131088 | tf_op jit(solution)/shard_map/psum | solution.py:40
  241.8 1.0 copy.15
  242.8 0.9 fusion.14
  243.8 11.7 %cholesky.50 = f32[128,128]{1,0:T(8,128)S(1)} custom-call(f32[128,128]{1,0:T(8,128)S(1)} %cholesky.118), custom_call_target="Cholesky" | custom-call | tf_op jit(solution)/shard_map/jit(cholesky)/cholesky | solution.py:41
  255.5 9.8 %custom-call.18 = f32[1,128,128]{1,2,0:T(8,128)S(1)} custom-call(f32[1,128,128]{2,1,0:T(8,128)S(1)} %get-tuple-element.32), custom_call_target="InvertDiagBlocksLowerTriangular" | custom-call | tf_op jit(solution)/shard_map/jit(cholesky)/cholesky | solution.py:41
  265.4 0.2 constant_dynamic-update-slice_fusion.1
  265.6 0.3 convolution_subtract_fusion.1
  265.8 11.7 %cholesky.105 = f32[128,128]{1,0:T(8,128)S(1)} custom-call(f32[128,128]{1,0:T(8,128)S(1)} %convolution_subtract_fusion.1), custom_call_target="Cholesky" | custom-call | tf_op jit(solution)/shard_map/jit(cholesky)/cholesky | solution.py:41
  277.6 0.6 compare_reduce_fusion
  279.6 0.8 copy.17
  280.4 0.1 triangular_solve.53
  280.5 3.8 %while.1 = (s32[]{:T(128)}, f32[256,256]{1,0:T(8,128)S(1)}, s32[2,2]{1,0:T(2,128)S(1)}, f32[2,128,128]{2,1,0:T(8,128)S(1)}, s32[]{:T(128)}) while((s32[]{:T(128)}, f32[256,256]{1,0:T(8,128)S(1)}, s32[2,2]{1,0:T(2,128)S(1)}, f32[2,128,128]{2,1,0:T(8,128)S(1)}, s32[]{:T(128)}) %tuple.31), condition=%wide.while_cond, body=%wide.while_body.sunk | while | flops 2 | bytes 131189 | solution.py:47
  280.5 0.6 fusion.37
  281.1 1.3 bitcast_dynamic-update-slice_fusion.2
  282.4 0.6 fusion.37
  283.0 1.3 bitcast_dynamic-update-slice_fusion.2
  284.3 19.8 %custom-call.19 = f32[2,128,128]{1,2,0:T(8,128)S(1)} custom-call(f32[2,128,128]{2,1,0:T(8,128)S(1)} %get-tuple-element.10), custom_call_target="InvertDiagBlocksLowerTriangular" | custom-call | tf_op jit(solution)/shard_map/jit(_solve_triangular)/triangular_solve | solution.py:47
  304.2 0.0 copy-start
  304.2 0.0 collective-permute-done.2
  304.2 4.0 %add_bitcast_fusion = f32[256,4096]{0,1:T(8,128)S(1)} fusion(f32[4096,256]{1,0:T(8,128)} %add.46, f32[4096,256]{1,0:T(8,128)} %collective-permute-done.2), kind=kLoop, calls=%fused_computation.14 | loop fusion | flops 1048576 | bytes 12582912 | tf_op jit(solution)/shard_map/transpose | solution.py:47
  308.2 2.0 fusion.8
  310.2 3.4 fusion.22
  313.7 2.1 fusion.7
  315.7 0.0 copy-done
  315.7 1.9 fusion.28
  317.6 2.4 maximum_bitcast_fusion
  320.0 0.0 copy-start.1
  320.0 2.2 convolution_subtract_fusion
  322.2 0.0 copy-done.1
  322.2 1.9 convolution_convert_fusion
  324.1 5.6 %copy.18 = f32[4096,256]{1,0:T(8,128)} copy(f32[4096,256]{0,1:T(8,128)} %maximum_bitcast_fusion) | data formatting | bytes 8388608
  329.7 19.1 %subtract_convert_fusion = bf16[2816,4096]{1,0:T(8,128)(2,1)} fusion(bf16[2816,4096]{1,0:T(8,128)(2,1)} %bitcast_select_fusion, bf16[2816,256]{1,0:T(8,128)(2,1)S(1)} %bitcast_select_fusion.1, bf16[128,4096]{1,0:T(8,128)(2,1)S(1)} %get-tuple-element.35, bf16[128,4096]{1,0:T(8,128)(2,1)S(1)} %convolution_convert_fusion), kind=kOutput, calls=%fused_computation.4 | convolution fusion | flops 5944377344 | bytes 49676288 | tf_op jit(solution)/shard_map/dot_general | solution.py:51
  (11 shorter events, 0.2 us)
Async XLA Ops:
  7.2 42.2 %all-gather.2.cloned.1.call-start = ((), (), s32[]{:S(2)}) async-start(), calls=%async_computation | async-start | bytes 1966080 | tf_op jit(solution)/shard_map/all_gather | solution.py:34
  7.9 233.9 %all-reduce.3.cloned.1.call-start = ((), (), s32[]{:S(2)}) async-start(), calls=%async_computation.1 | async-start | bytes 262144 | tf_op jit(solution)/shard_map/psum | solution.py:40
  8.6 17.7 %copy-start.2 = (s32[22]{0:T(128)S(1)}, s32[22]{0:T(128)}, u32[]{:S(2)}) copy-start(s32[22]{0:T(128)} %param.5) | copy-start | bytes 268
  63.5 7.2 %collective-permute-start = (f32[4096,256]{1,0:T(8,128)S(1)}, f32[4096,256]{1,0:T(8,128)S(1)}, u32[]{:S(2)}, u32[]{:S(2)}) collective-permute-start(f32[4096,256]{1,0:T(8,128)S(1)} %fusion.4), channel_id=1, source_target_pairs={{0,4},{4,0},{8,12},{12,8},{16,20},{20,16},{24,28},{28,24},{1,5},{5... | collective-permute-start | bytes 12582920 | tf_op jit(solution)/shard_map/ppermute | solution.py:20
  71.3 92.7 %collective-permute-start.1 = (f32[4096,256]{1,0:T(8,128)S(1)}, f32[4096,256]{1,0:T(8,128)S(1)}, u32[]{:S(2)}, u32[]{:S(2)}) collective-permute-start(f32[4096,256]{1,0:T(8,128)S(1)} %add.45), channel_id=1, source_target_pairs={{0,8},{4,12},{8,0},{12,4},{16,24},{20,28},{24,16},{28,20},{1,9},{5... | collective-permute-start | bytes 12582920 | tf_op jit(solution)/shard_map/ppermute | solution.py:20
  166.5 137.6 %collective-permute-start.2 = (f32[4096,256]{1,0:T(8,128)}, f32[4096,256]{1,0:T(8,128)}, u32[]{:S(2)}, u32[]{:S(2)}) collective-permute-start(f32[4096,256]{1,0:T(8,128)} %add.46), channel_id=1, source_target_pairs={{0,16},{4,20},{8,24},{12,28},{16,0},{20,4},{24,8},{28,12},{1,17},{... | collective-permute-start | bytes 12582920 | tf_op jit(solution)/shard_map/ppermute | solution.py:20
  304.2 11.6 %copy-start = (f32[2,128,128]{1,2,0:T(8,128)}, f32[2,128,128]{1,2,0:T(8,128)S(1)}, u32[]{:S(2)}) copy-start(f32[2,128,128]{1,2,0:T(8,128)S(1)} %custom-call.19) | copy-start | bytes 393220
  320.0 2.2 copy-start.1
Sparse Core Ops, SparseCore 0:
  9.5 39.7 all-gather.1
  190.2 51.5 all-reduce.2
